TPU v7x, 32 devices: a whole 2x2x4 slice. The times are simulated.
32 devices in a mesh: seq: 8 (over z, y), dp: 4 (over x, core).
Axes of the slice: x: 2, y: 2, z: 4, core: 2. Of those that a mesh axis runs over, the one named last changes fastest.
Arguments:
- tokens: bfloat16 [4, 2048, 2048], P('dp', 'seq'), may hold values from -6 to 6
- query_weight: bfloat16 [2048, 2048], P(None, 'seq'), may hold values from -0.125 to 0.125
- key_rows: bfloat16 [4, 2048, 2048], P('dp', 'seq'), may hold values from -6 to 6
- value_rows: bfloat16 [4, 2048, 2048], P('dp', 'seq'), may hold values from -6 to 6
- out_grad: bfloat16 [4, 2048, 2048], P('dp', 'seq'), may hold values from -6 to 6
Outputs:
- attended: bfloat16 [4, 2048, 2048], P('dp', 'seq')
- key_grad: bfloat16 [4, 2048, 2048], P('dp', 'seq')
- value_grad: bfloat16 [4, 2048, 2048], P('dp', 'seq')
- weight_grad: float32 [2048, 2048], P('seq')
All inputs are finite; a program needn't handle non-finite values.
Results may differ from a plain program's by a relative error of at most 0.0058.
Values may be sent and summed in bfloat16 or wider, within the bound.
No kernel may reach another device: no remote copies, remote signals or barrier semaphores. Data moves between devices by JAX's collectives and lax.ppermute only.
A program may use at most 320 MiB of HBM per device.

v0:
```python
import math
import jax
import jax.numpy as jnp
from jax import lax
from jax.sharding import PartitionSpec as P

DH = 128


def carried_in(value, axis, join, neutral, backward):
    count, mine = (lax.axis_size(axis), lax.axis_index(axis))
    pieces = lax.all_gather(value, axis)
    if backward:
        pieces = pieces[::-1]
        mine = count - 1 - mine
    total = jnp.full_like(value, 0) + jnp.asarray(neutral, value.dtype)

    def step(position, total):
        longer = join(total, pieces[position])
        return jnp.where(position < mine, longer, total)

    return lax.fori_loop(0, count - 1, step, total)


def pair_sum(earlier, later):
    return jax.tree.map(jnp.add, earlier, later)


def body(tokens, query_weight, key_rows, value_rows, out_grad):
    row_count = tokens.shape[1]
    hidden_width = key_rows.shape[2]
    head_count = hidden_width // DH
    seq_count = lax.axis_size("seq")
    factor = 1.0 / math.sqrt(DH * row_count * seq_count)
    local_tokens = tokens[0]
    query_rows = jnp.dot(
        local_tokens,
        lax.all_gather(query_weight, "seq", axis=1, tiled=True),
        preferred_element_type=jnp.float32,
    ).astype(jnp.bfloat16)
    query_heads = query_rows.reshape(row_count, head_count, DH)
    key_heads = key_rows[0].reshape(row_count, head_count, DH)
    value_heads = value_rows[0].reshape(row_count, head_count, DH)
    grad_heads = out_grad[0].reshape(row_count, head_count, DH)
    block_kv = jnp.einsum(
        "rhd,rhe->hde", key_heads, value_heads, preferred_element_type=jnp.float32
    )
    block_qg = jnp.einsum(
        "rhd,rhe->hde", query_heads, grad_heads, preferred_element_type=jnp.float32
    )
    zero_state = jnp.zeros_like(block_kv)
    prefix_state = carried_in(block_kv, "seq", pair_sum, zero_state, False)
    suffix_state = carried_in(block_qg, "seq", pair_sum, zero_state, True)
    prefix_half = prefix_state.astype(jnp.bfloat16)
    suffix_half = suffix_state.astype(jnp.bfloat16)
    lower_mask = (
        lax.broadcasted_iota(jnp.int32, (row_count, row_count), 0)
        >= lax.broadcasted_iota(jnp.int32, (row_count, row_count), 1)
    )[None]
    key_scores = jnp.where(
        lower_mask,
        factor
        * jnp.einsum("ihd,jhd->hij", query_heads, key_heads, preferred_element_type=jnp.float32),
        0.0,
    ).astype(jnp.bfloat16)
    grad_scores = jnp.where(
        lower_mask,
        factor
        * jnp.einsum("ihe,jhe->hij", grad_heads, value_heads, preferred_element_type=jnp.float32),
        0.0,
    ).astype(jnp.bfloat16)
    attended = jnp.einsum(
        "hij,jhe->ihe", key_scores, value_heads, preferred_element_type=jnp.float32
    ) + factor * jnp.einsum(
        "ihd,hde->ihe", query_heads, prefix_half, preferred_element_type=jnp.float32
    )
    query_grad = jnp.einsum(
        "hij,jhd->ihd", grad_scores, key_heads, preferred_element_type=jnp.float32
    ) + factor * jnp.einsum(
        "ihe,hde->ihd", grad_heads, prefix_half, preferred_element_type=jnp.float32
    )
    key_grad = jnp.einsum(
        "hij,ihd->jhd", grad_scores, query_heads, preferred_element_type=jnp.float32
    ) + factor * jnp.einsum(
        "jhe,hde->jhd", value_heads, suffix_half, preferred_element_type=jnp.float32
    )
    value_grad = jnp.einsum(
        "hij,ihe->jhe", key_scores, grad_heads, preferred_element_type=jnp.float32
    ) + factor * jnp.einsum(
        "jhd,hde->jhe", key_heads, suffix_half, preferred_element_type=jnp.float32
    )
    attended = attended.reshape(1, row_count, hidden_width).astype(jnp.bfloat16)
    query_grad = query_grad.reshape(row_count, hidden_width).astype(jnp.bfloat16)
    key_grad = key_grad.reshape(1, row_count, hidden_width).astype(jnp.bfloat16)
    value_grad = value_grad.reshape(1, row_count, hidden_width).astype(jnp.bfloat16)
    grad_shard = lax.psum_scatter(
        lax.dot_general(
            local_tokens, query_grad, (((0,), (0,)), ((), ())), preferred_element_type=jnp.float32
        ),
        "seq",
        scatter_dimension=0,
        tiled=True,
    )
    weight_grad = lax.psum(grad_shard, "dp")
    return (attended, key_grad, value_grad, weight_grad)


def solution(mesh):
    return jax.shard_map(
        body,
        mesh=mesh,
        in_specs=(
            P("dp", "seq", None),
            P(None, "seq"),
            P("dp", "seq", None),
            P("dp", "seq", None),
            P("dp", "seq", None),
        ),
        out_specs=(
            P("dp", "seq", None),
            P("dp", "seq", None),
            P("dp", "seq", None),
            P("seq", None),
        ),
        check_vma=False,
    )
```

profile of v0, /device:TPU:0, one launch (start us, length us, event | category | flops | bytes accessed | tf_op | source)
XLA Modules:
  0.0 732.2 jit_solution(10739160041827640124)
XLA Ops:
  13.8 2.5 copy.58
  16.3 121.4 %all-gather.6.cloned.1.call-done = bf16[2048,2048]{1,0:T(8,128)(2,1)} async-done(((bf16[2048,256]{1,0:T(8,128)(2,1)}), bf16[2048,2048]{1,0:T(8,128)(2,1)}) %all-gather.6.cloned.1.call-update) | async-done | bytes 8388624 | tf_op jit(solution)/shard_map/all_gather | solution.py:38
  137.7 6.7 convolution_convert_fusion
  145.9 3.2 fusion.11
  149.3 2.1 select_convert_fusion
  152.8 2.2 fusion.24
  155.0 108.1 %all-gather.8.cloned.1.call-done = f32[128,128,128]{2,1,0:T(8,128)} async-done(((f32[16,128,128]{2,1,0:T(8,128)}), f32[128,128,128]{2,1,0:T(8,128)}) %all-gather.8.cloned.1.call-update) | async-done | bytes 8388624 | tf_op jit(solution)/shard_map/all_gather | solution.py:12
  263.1 11.6 %while.28 = (s32[]{:T(128)}, f32[16,128,128]{2,1,0:T(8,128)S(1)}, s32[]{:T(128)}, f32[8,16,128,128]{3,2,1,0:T(8,128)}, s32[]{:T(128)}, /*index=5*/s32[]{:T(128)}) while((s32[]{:T(128)}, f32[16,128,128]{2,1,0:T(8,128)S(1)}, s32[]{:T(128)}, f32[8,16,128,128]{3,2,1,0:T(8,128)}, s32[]{:T(128)}, /*index=5*/s32[]{:T(128)}) %tuple.81), condition=%wide.region_1.2_spmd.clone, body=%wide.region_0.1_spmd.clone.sunk | while | flops 786436 | bytes 3145821 | solution.py:22
  269.6 1.7 add_select_fusion.4
  271.3 1.7 add_select_fusion.4
  273.0 1.7 add_select_fusion.4
  274.8 2.4 fusion
  277.2 8.1 %convolution_bitcast_fusion = f32[2048,2048]{0,1:T(8,128)} fusion(bf16[256,2048]{0,1:T(8,128)(2,1)S(1)} %bitcast.79, bf16[1,256,2048]{2,1,0:T(8,128)(2,1)S(1)} %copy-done), kind=kOutput, calls=%fused_computation.2 | convolution fusion | flops 2147483648 | bytes 18874368 | tf_op jit(solution)/shard_map/dot_general | solution.py:97
  285.6 2.4 select_convert_fusion.1
  291.5 2.4 copy.49
  293.8 3.4 fusion.23
  297.2 90.8 %all-gather.10.cloned.1.call-done = f32[128,128,128]{2,1,0:T(8,128)} async-done(((f32[16,128,128]{2,1,0:T(8,128)}), f32[128,128,128]{2,1,0:T(8,128)}) %all-gather.10.cloned.1.call-update) | async-done | bytes 8388624 | tf_op jit(solution)/shard_map/all_gather | solution.py:12
  387.9 7.7 %rev.3 = f32[8,16,128,128]{3,2,1,0:T(8,128)} reverse(f32[8,16,128,128]{3,2,1,0:T(8,128)} %bitcast.78), dimensions={0} | reverse | bytes 16777216 | tf_op jit(solution)/shard_map/rev | solution.py:14
  395.7 11.4 %while.29 = (s32[]{:T(128)}, f32[16,128,128]{2,1,0:T(8,128)S(1)}, s32[]{:T(128)}, f32[8,16,128,128]{3,2,1,0:T(8,128)}, s32[]{:T(128)}, /*index=5*/s32[]{:T(128)}) while((s32[]{:T(128)}, f32[16,128,128]{2,1,0:T(8,128)S(1)}, s32[]{:T(128)}, f32[8,16,128,128]{3,2,1,0:T(8,128)}, s32[]{:T(128)}, /*index=5*/s32[]{:T(128)}) %tuple.68), condition=%wide.region_3.4_spmd.clone, body=%wide.region_2.3_spmd.clone.sunk | while | flops 786436 | bytes 3145821 | solution.py:22
  407.1 263.0 %reduce-scatter.2.cloned.1.call-done = f32[256,2048]{0,1:T(8,128)} async-done(((f32[2048,2048]{0,1:T(8,128)}), f32[256,2048]{0,1:T(8,128)}) %reduce-scatter.2.cloned.1.call-update) | async-done | bytes 2097168 | tf_op jit(solution)/shard_map/reduce_scatter | solution.py:96
  670.1 3.1 add_convert_fusion
  673.2 2.4 copy.50
  679.9 43.0 %all-reduce.2.cloned.1.call-done = f32[256,2048]{0,1:T(8,128)} async-done(((f32[256,2048]{0,1:T(8,128)}), f32[256,2048]{0,1:T(8,128)}) %all-reduce.2.cloned.1.call-update) | async-done | bytes 2097168 | tf_op jit(solution)/shard_map/psum | solution.py:104
  722.8 2.9 copy.52
  (60 shorter events, 35.0 us)
Async XLA Ops:
  7.2 130.6 %copy-start = (bf16[1,256,2048]{2,1,0:T(8,128)(2,1)S(1)}, bf16[1,256,2048]{2,1,0:T(8,128)(2,1)}, u32[]{:S(2)}) copy-start(bf16[1,256,2048]{2,1,0:T(8,128)(2,1)} %param.9) | copy-start | bytes 3145732
  7.2 2.3 copy-start.12
  7.2 130.5 %all-gather.6.cloned.1.call-start = ((), (), s32[]{:S(2)}) async-start(), calls=%async_computation.1 | async-start | bytes 9437184 | tf_op jit(solution)/shard_map/all_gather | solution.py:38
  7.9 255.2 %all-gather.8.cloned.1.call-start = ((), (), s32[]{:S(2)}) async-start(), calls=%async_computation.4 | async-start | bytes 9437184 | tf_op jit(solution)/shard_map/all_gather | solution.py:12
  12.3 1.5 copy-start.6
  13.8 374.2 %all-gather.10.cloned.1.call-start = ((), (), s32[]{:S(2)}) async-start(), calls=%async_computation.5 | async-start | bytes 9437184 | tf_op jit(solution)/shard_map/all_gather | solution.py:12
  145.9 3.3 copy-start.2
  149.2 520.9 %reduce-scatter.2.cloned.1.call-start = ((), (), s32[]{:S(2)}) async-start(), calls=%async_computation.2 | async-start | bytes 18874368 | tf_op jit(solution)/shard_map/reduce_scatter | solution.py:96
  149.3 3.5 copy-start.7
  151.5 1.3 copy-start.11
  285.3 437.5 %all-reduce.2.cloned.1.call-start = ((), (), s32[]{:S(2)}) async-start(), calls=%async_computation.3 | async-start | bytes 4194304 | tf_op jit(solution)/shard_map/psum | solution.py:104
  288.0 1.4 copy-start.9
  288.0 2.0 copy-start.3
  291.5 2.4 copy-start.4
  673.2 2.4 copy-start.8
  675.5 1.3 copy-start.5
  675.5 2.3 copy-start.10
  678.4 47.3 %copy-start.1 = (bf16[1,256,2048]{2,1,0:T(8,128)(2,1)S(1)}, bf16[1,256,2048]{2,1,0:T(8,128)(2,1)}, u32[]{:S(2)}) copy-start(bf16[1,256,2048]{2,1,0:T(8,128)(2,1)} %param.9) | copy-start | bytes 3145732
Sparse Core Ops, SparseCore 0:
  10.0 127.6 all-gather.5
  140.4 122.6 all-gather.7
  265.3 122.6 all-gather.9
  391.6 278.4 reduce-scatter.1
  672.3 50.4 all-reduce.1
where the time goes:
time: 733 us; the launch traced here: 732 us
  waiting for transfers between devices  627 us (86%)
  matrix products  38.5 us (5%)
  local copies, waits for them, and re-layouts  29.3 us (4%)
  other arithmetic  22.7 us (3%)
  between operations  14 us (2%)
    reduce_scatter x1, waiting for transfers between devices, body(): lax.psum_scatter(lax.dot_general(local_tokens, query_grad, (((0,), (0,)),...  263 us
    all_gather x2, waiting for transfers between devices, carried_in(): pieces = lax.all_gather(value, axis)  199 us
    all_gather x1, waiting for transfers between devices, body(): lax.all_gather(query_weight, 'seq', axis=1, tiled=True)  121 us
    psum x1, waiting for transfers between devices, body(): weight_grad = lax.psum(grad_shard, 'dp')  43 us
    select_n x14, other arithmetic, step(): return jnp.where(position < mine, longer, total)  22.7 us
    unnamed x33, local copies, waits for them, and re-layouts  18.5 us
  transfers between devices with their start and end apart: 5, of which 5 were waited for; matrix products, arithmetic and copies ran while one was open for 11% of the time, Pallas kernels for 0%

commit v1 on v0

--- a/solution.py
+++ b/solution.py
@@ -5,6 +5,11 @@
 from jax.sharding import PartitionSpec as P
 
 DH = 128
+
+
+def add_all(value, axis):
+    shards = lax.all_gather(value, axis)
+    return jnp.sum(shards, axis=0)
 
 
 def carried_in(value, axis, join, neutral, backward):
@@ -101,7 +106,7 @@
         scatter_dimension=0,
         tiled=True,
     )
-    weight_grad = lax.psum(grad_shard, "dp")
+    weight_grad = add_all(grad_shard, "dp")
     return (attended, key_grad, value_grad, weight_grad)
 
 

time: 733 us -> 767 us (1.046)
  other arithmetic: 22.7 us -> 36.7 us
  local copies, waits for them, and re-layouts: 29.3 us -> 40.5 us
  waiting for transfers between devices: 627 us -> 635 us
    psum x1 -> x0, waiting for transfers between devices: 43 us -> none  [body(): weight_grad = lax.psum(grad_shard, 'dp')]
    all_gather x2, waiting for transfers between devices: 199 us -> 232 us  [carried_in(): pieces = lax.all_gather(value, axis)]
    all_gather x0 -> x1, waiting for transfers between devices: none -> 28.3 us  [add_all(): shards = lax.all_gather(value, axis)]
    all_gather x1, waiting for transfers between devices: 121 us -> 103 us  [body(): lax.all_gather(query_weight, 'seq', axis=1, tiled=True)]
    reduce_sum x0 -> x1, other arithmetic: none -> 13.8 us  [add_all(): return jnp.sum(shards, axis=0)]
    all_gather x0 -> x1, local copies, waits for them, and re-layouts: none -> 10.5 us  [add_all(): shards = lax.all_gather(value, axis)]
  transfers between devices with their start and end apart: 5 -> 5, of which waited for: 5 -> 5; matrix products, arithmetic and copies ran while one was open for 11% -> 10% of each run, Pallas kernels for 0% -> 0%
where the time goes in v1:
time: 767 us; the launch traced here: 765 us
  waiting for transfers between devices  635 us (83%)
  local copies, waits for them, and re-layouts  40.5 us (5%)
  matrix products  38.8 us (5%)
  other arithmetic  36.7 us (5%)
  between operations  14 us (2%)
    reduce_scatter x1, waiting for transfers between devices, body(): lax.psum_scatter(lax.dot_general(local_tokens, query_grad, (((0,), (0,)),...  271 us
    all_gather x2, waiting for transfers between devices, carried_in(): pieces = lax.all_gather(value, axis)  232 us
    all_gather x1, waiting for transfers between devices, body(): lax.all_gather(query_weight, 'seq', axis=1, tiled=True)  103 us
    all_gather x1, waiting for transfers between devices, add_all(): shards = lax.all_gather(value, axis)  28.3 us
    select_n x14, other arithmetic, step(): return jnp.where(position < mine, longer, total)  22.8 us
    unnamed x33, local copies, waits for them, and re-layouts  18.2 us
  transfers between devices with their start and end apart: 5, of which 5 were waited for; matrix products, arithmetic and copies ran while one was open for 10% of the time, Pallas kernels for 0%

profile of v1, /device:TPU:0, one launch (start us, length us, event | category | flops | bytes accessed | tf_op | source)
XLA Modules:
  0.0 765.3 jit_solution(17214335834725478975)
XLA Ops:
  14.0 2.5 copy.57
  16.5 2.1 select_convert_fusion
  20.0 2.2 fusion.24
  22.2 118.3 %all-gather.10.cloned.1.call-done = f32[128,128,128]{2,1,0:T(8,128)} async-done(((f32[16,128,128]{2,1,0:T(8,128)}), f32[128,128,128]{2,1,0:T(8,128)}) %all-gather.10.cloned.1.call-update) | async-done | bytes 8388624 | tf_op jit(solution)/shard_map/all_gather | solution.py:17
  140.5 11.5 %while.28 = (s32[]{:T(128)}, f32[16,128,128]{2,1,0:T(8,128)S(1)}, s32[]{:T(128)}, f32[8,16,128,128]{3,2,1,0:T(8,128)}, s32[]{:T(128)}, /*index=5*/s32[]{:T(128)}) while((s32[]{:T(128)}, f32[16,128,128]{2,1,0:T(8,128)S(1)}, s32[]{:T(128)}, f32[8,16,128,128]{3,2,1,0:T(8,128)}, s32[]{:T(128)}, /*index=5*/s32[]{:T(128)}) %tuple.81), condition=%wide.region_1.2_spmd.clone, body=%wide.region_0.1_spmd.clone.sunk | while | flops 786436 | bytes 3145821 | solution.py:27
  152.1 2.5 fusion
  154.6 8.1 %convolution_bitcast_fusion = f32[2048,2048]{0,1:T(8,128)} fusion(bf16[256,2048]{0,1:T(8,128)(2,1)S(1)} %bitcast.81, bf16[1,256,2048]{2,1,0:T(8,128)(2,1)S(1)} %copy-done), kind=kOutput, calls=%fused_computation.2 | convolution fusion | flops 2147483648 | bytes 18874368 | tf_op jit(solution)/shard_map/dot_general | solution.py:102
  162.7 103.0 %all-gather.8.cloned.1.call-done = bf16[2048,2048]{1,0:T(8,128)(2,1)} async-done(((bf16[2048,256]{1,0:T(8,128)(2,1)}), bf16[2048,2048]{1,0:T(8,128)(2,1)}) %all-gather.8.cloned.1.call-update) | async-done | bytes 8388624 | tf_op jit(solution)/shard_map/all_gather | solution.py:43
  265.7 6.7 convolution_convert_fusion
  273.9 3.3 fusion.11
  277.4 270.6 %reduce-scatter.2.cloned.1.call-done = f32[256,2048]{0,1:T(8,128)} async-done(((f32[2048,2048]{0,1:T(8,128)}), f32[256,2048]{0,1:T(8,128)}) %reduce-scatter.2.cloned.1.call-update) | async-done | bytes 2097168 | tf_op jit(solution)/shard_map/reduce_scatter | solution.py:101
  548.1 2.4 select_convert_fusion.1
  554.0 2.4 copy.48
  556.3 3.6 fusion.23
  559.9 113.7 %all-gather.12.cloned.1.call-done = f32[128,128,128]{2,1,0:T(8,128)} async-done(((f32[16,128,128]{2,1,0:T(8,128)}), f32[128,128,128]{2,1,0:T(8,128)}) %all-gather.12.cloned.1.call-update) | async-done | bytes 8388624 | tf_op jit(solution)/shard_map/all_gather | solution.py:17
  673.6 8.6 %rev.3 = f32[8,16,128,128]{3,2,1,0:T(8,128)} reverse(f32[8,16,128,128]{3,2,1,0:T(8,128)} %bitcast.80), dimensions={0} | reverse | bytes 16777216 | tf_op jit(solution)/shard_map/rev | solution.py:19
  682.2 11.6 %while.29 = (s32[]{:T(128)}, f32[16,128,128]{2,1,0:T(8,128)S(1)}, s32[]{:T(128)}, f32[8,16,128,128]{3,2,1,0:T(8,128)}, s32[]{:T(128)}, /*index=5*/s32[]{:T(128)}) while((s32[]{:T(128)}, f32[16,128,128]{2,1,0:T(8,128)S(1)}, s32[]{:T(128)}, f32[8,16,128,128]{3,2,1,0:T(8,128)}, s32[]{:T(128)}, /*index=5*/s32[]{:T(128)}) %tuple.68), condition=%wide.region_3.4_spmd.clone, body=%wide.region_2.3_spmd.clone.sunk | while | flops 786436 | bytes 3145821 | solution.py:27
  682.2 1.7 add_select_fusion.5
  693.9 3.1 add_convert_fusion
  696.9 2.4 copy.49
  703.3 28.3 %all-gather.14.cloned.1.call-done = f32[1024,2048]{0,1:T(8,128)} async-done(((f32[256,2048]{0,1:T(8,128)}), f32[1024,2048]{0,1:T(8,128)}) %all-gather.14.cloned.1.call-update) | async-done | bytes 8388624 | tf_op jit(solution)/shard_map/all_gather | solution.py:11
  731.5 10.5 %reshape.65 = f32[4,256,2048]{1,0,2:T(4,128)} reshape(f32[1024,2048]{0,1:T(8,128)} %all-gather.14.cloned.1.call-done) | data formatting | bytes 16777216 | tf_op jit(solution)/shard_map/all_gather | solution.py:11
  742.1 13.8 %reduce_sum.9 = f32[256,2048]{0,1:T(8,128)} reduce(f32[4,256,2048]{1,0,2:T(4,128)} %reshape.65, f32[]{:T(128)} %constant.55.clone.1), dimensions={0}, to_apply=%region_5.6 | reduce | flops 1572864 | bytes 10485764 | tf_op jit(solution)/shard_map/reduce_sum | solution.py:12
  755.9 2.9 copy.51
  (62 shorter events, 38.4 us)
Async XLA Ops:
  7.2 147.4 %copy-start = (bf16[1,256,2048]{2,1,0:T(8,128)(2,1)S(1)}, bf16[1,256,2048]{2,1,0:T(8,128)(2,1)}, u32[]{:S(2)}) copy-start(bf16[1,256,2048]{2,1,0:T(8,128)(2,1)} %param.9) | copy-start | bytes 3145732
  7.2 1.7 copy-start.12
  7.2 133.3 %all-gather.10.cloned.1.call-start = ((), (), s32[]{:S(2)}) async-start(), calls=%async_computation.3 | async-start | bytes 9437184 | tf_op jit(solution)/shard_map/all_gather | solution.py:17
  11.7 1.5 copy-start.6
  13.2 252.5 %all-gather.8.cloned.1.call-start = ((), (), s32[]{:S(2)}) async-start(), calls=%async_computation.1 | async-start | bytes 9437184 | tf_op jit(solution)/shard_map/all_gather | solution.py:43
  14.0 534.1 %reduce-scatter.2.cloned.1.call-start = ((), (), s32[]{:S(2)}) async-start(), calls=%async_computation.2 | async-start | bytes 18874368 | tf_op jit(solution)/shard_map/reduce_scatter | solution.py:101
  16.5 3.5 copy-start.7
  18.7 1.3 copy-start.11
  162.7 511.0 %all-gather.12.cloned.1.call-start = ((), (), s32[]{:S(2)}) async-start(), calls=%async_computation.4 | async-start | bytes 9437184 | tf_op jit(solution)/shard_map/all_gather | solution.py:17
  273.9 3.3 copy-start.2
  277.2 454.3 %all-gather.14.cloned.1.call-start = ((), (), s32[]{:S(2)}) async-start(), calls=%async_computation.5 | async-start | bytes 10485760 | tf_op jit(solution)/shard_map/all_gather | solution.py:11
  550.5 1.4 copy-start.9
  550.5 2.0 copy-start.3
  554.0 2.4 copy-start.4
  696.9 2.4 copy-start.8
  699.3 1.2 copy-start.5
  699.3 1.9 copy-start.10
  742.1 16.7 %copy-start.1 = (bf16[1,256,2048]{2,1,0:T(8,128)(2,1)S(1)}, bf16[1,256,2048]{2,1,0:T(8,128)(2,1)}, u32[]{:S(2)}) copy-start(bf16[1,256,2048]{2,1,0:T(8,128)(2,1)} %param.9) | copy-start | bytes 3145732
Sparse Core Ops, SparseCore 0:
  13.3 127.1 all-gather.9
  142.6 123.1 all-gather.7
  269.5 278.4 reduce-scatter.1
  550.0 123.5 all-gather.11
  675.0 56.4 all-gather.13
